TPU v7x, 32 devices: a whole 2x2x4 slice. The times are simulated.
32 devices in a mesh: grp: 2 (over y), doc: 4 (over x, core), voc: 4 (over z).
Axes of the slice: x: 2, y: 2, z: 4, core: 2. Of those that a mesh axis runs over, the one named last changes fastest.
Arguments:
- hidden: bfloat16 [48, 256, 768], P(('grp', 'doc')), parts along dimension 0, may hold values from -6 to 6
- lengths: int32 [48], P(('grp', 'doc')), parts along dimension 0, may hold values from 1 to 256, 3840 in all
- w_trans: bfloat16 [768, 768], replicated, may hold values from -0.21875 to 0.21875
- b_trans: float32 [768], replicated, may hold values from -3 to 3
- ln_gain: float32 [768], replicated, may hold values from 0.5 to 1.5
- ln_bias: float32 [768], replicated, may hold values from -3 to 3
- w_decode: bfloat16 [768, 30720], P(None, 'voc'), may hold values from -0.21875 to 0.21875
- b_decode: float32 [30720], P('voc'), may hold values from -5 to 5
- query_ids: int32 [2048, 32], P('grp'), parts along dimension 0, may hold values from 0 to 30719
- query_wts: int32 [2048, 32], P('grp'), parts along dimension 0, may hold values from 1 to 100
Outputs:
- scores: float32 [48, 1024], P(('grp', 'voc'), 'doc'), parts along dimension 0
There are 2 independent parts, one for each index of `grp`. A program takes and returns all parts, laid end to end along the dimension named above; an argument that names none is the same for every part. Nothing has to cross between parts.
Inputs may be any that keep to these rules, and one draw needn't show every extreme that they name: Every passage has at least one live token and the longest has exactly 256. Within each grp group the 24 lengths sum to 3840; over the whole array, which holds both groups, the sum is twice that.
All inputs are finite; a program needn't handle non-finite values.
Results may differ from a plain program's by a relative error of at most 0.0003.
Values sent between devices are 32-bit elements; how exact they have to be, the bound alone decides.
A program may use at most 64 MiB of HBM per device.

v0:
```python
import jax
import jax.numpy as jnp
from jax import lax
from jax.sharding import PartitionSpec as P

eps = 1e-06
score_scale = 1.0 / 1024.0
dead_fill = -1e30


def transform(hidden, w_trans, b_trans, ln_gain, ln_bias):
    count, length, width = hidden.shape
    flat = hidden.reshape(count * length, width)
    pre = jnp.dot(flat, w_trans, preferred_element_type=jnp.float32) + b_trans
    active = jax.nn.gelu(pre, approximate=False)
    centre = active - jnp.mean(active, -1, keepdims=True)
    spread = jnp.mean(centre * centre, -1, keepdims=True)
    normed = centre * lax.rsqrt(spread + eps) * ln_gain + ln_bias
    return normed.astype(jnp.bfloat16).reshape(count, length, width)


def block_terms(query_ids, query_wts, start, width):
    local_ids = query_ids - start
    inside = (local_ids >= 0) & (local_ids < width)
    clipped = jnp.clip(local_ids, 0, width - 1)
    weights = jnp.where(inside, query_wts, 0).astype(jnp.float32)
    return (clipped, weights)


def score_rows(rows, local_ids, weights):
    picked = rows[:, local_ids]
    return jnp.sum(picked * weights[None], -1) * score_scale


def shards(
    hidden, lengths, w_trans, b_trans, ln_gain, ln_bias, w_decode, b_decode, query_ids, query_wts
):
    transformed = transform(hidden, w_trans, b_trans, ln_gain, ln_bias)

    def pool_rows(pair):
        passage, live = pair
        logits = jnp.dot(passage, w_decode, preferred_element_type=jnp.float32) + b_decode
        inside = jnp.arange(passage.shape[0], dtype=jnp.int32)[:, None] < live
        top = jnp.max(jnp.where(inside, logits, jnp.full_like(logits, dead_fill)), 0)
        return jnp.log1p(jnp.maximum(top, jnp.zeros_like(top)))

    impacts = lax.map(pool_rows, (transformed, lengths))
    term_width = w_decode.shape[1]
    term_start = lax.axis_index("voc") * term_width
    local_ids, weights = block_terms(query_ids, query_wts, term_start, term_width)
    own_count = query_ids.shape[0] // lax.axis_size("doc")
    own_start = lax.axis_index("doc") * own_count
    own_ids = lax.dynamic_slice_in_dim(local_ids, own_start, own_count, 0)
    own_weights = lax.dynamic_slice_in_dim(weights, own_start, own_count, 0)
    partial_value = score_rows(
        lax.all_gather(impacts, "doc", axis=0, tiled=True), own_ids, own_weights
    )
    return lax.psum_scatter(partial_value, "voc", scatter_dimension=0, tiled=True)


def solution(mesh):
    return jax.shard_map(
        shards,
        mesh=mesh,
        in_specs=(
            P(("grp", "doc"), None, None),
            P(("grp", "doc")),
            P(),
            P(),
            P(),
            P(),
            P(None, "voc"),
            P("voc"),
            P("grp", None),
            P("grp", None),
        ),
        out_specs=P(("grp", "voc"), "doc"),
        check_vma=False,
    )
```

profile of v0, /device:TPU:0, one launch (start us, length us, event | category | flops | bytes accessed | tf_op | source)
XLA Modules:
  0.0 166.4 jit_solution(11314544946530714694)
XLA Ops:
  0.0 1.1 broadcast_subtract_fusion
  1.1 0.8 compare_select_fusion
  1.9 0.1 copy.16
  2.0 0.1 reshape.45
  2.1 29.6 %fusion.16 = (f32[1536]{0:T(1024)S(1)}, f32[1536,768]{1,0:T(8,128)S(1)}) fusion(f32[768]{0:T(1024)} %param.15, bf16[1536,768]{1,0:T(8,128)(2,1)S(1)} %bitcast.23, bf16[768,768]{1,0:T(8,128)(2,1)} %param.14), kind=kOutput, calls=%fused_computation.39 | convolution fusion | flops 1889794560 | bytes 8266752 | tf_op jit(solution)/shard_map/dot_general | solution.py:14
  31.6 0.0 copy-start.1
  31.7 0.0 copy-start.2
  31.7 0.7 multiply_reduce_fusion
  32.4 0.0 copy-start.5
  32.4 2.1 %add_convert_fusion = bf16[1536,768]{1,0:T(8,128)(2,1)} fusion(f32[1536,768]{1,0:T(8,128)S(1)} %get-tuple-element.53, f32[768]{0:T(1024)S(1)} %copy-done.1, f32[768]{0:T(1024)S(1)} %copy-done.2, f32[1536]{0:T(1024)S(1)} %add_rsqrt_fusion, f32[1536]{0:T(1024)S(1)} %broadcast_multiply_fusion), kind=kLoop, calls=%fused_computation.12 | loop fusion | flops 5898240 | bytes 7096320 | tf_op jit(solution)/shard_map/convert_element_type | solution.py:19
  34.6 65.5 %while.10 = (s32[]{:T(128)}, f32[6,7680]{1,0:T(8,128)}, s32[6]{0:T(128)S(1)}, bf16[6,256,768]{2,1,0:T(8,128)(2,1)}, bf16[768,7680]{1,0:T(8,128)(2,1)}, /*index=5*/f32[7680]{0:T(1024)S(1)}, s32[]{:T(128)}, s32[]{:T(128)}) while((s32[]{:T(128)}, f32[6,7680]{1,0:T(8,128)}, s32[6]{0:T(128)S(1)}, bf16[6,256,768]{2,1,0:T(8,128)(2,1)}, ...), condition=%wide.region_4.5_spmd, body=%wide.region_2.4_spmd.sunk | while | flops 3025797376 | bytes 12436585 | solution.py:47
  34.6 0.7 dynamic_slice.31
  35.2 0.7 iota_compare_fusion.2
  35.9 7.7 %fusion.25 = f32[7680]{0:T(1024)S(1)} fusion(f32[7680]{0:T(1024)S(1)} %get-tuple-element.112, bf16[768,7680]{1,0:T(8,128)(2,1)} %get-tuple-element.111, pred[256]{0:T(512)(128)(4,1)S(1)} %iota_compare_fusion.2, bf16[6,256,768]{2,1,0:T(8,128)(2,1)} %get-tuple-element.110, s32[]{:T(128)} %get-tuple-element.99), kind=kOutput, calls=%fused_computation.3.clone.1 | convolution fusion | flops 3025789440 | bytes 12251904 | tf_op jit(solution)/shard_map/while/body/eval_jaxpr/dot_general | solution.py:42
  43.7 1.8 %dynamic_update_slice.5 = f32[6,7680]{1,0:T(8,128)} dynamic-update-slice(f32[6,7680]{1,0:T(8,128)} %get-tuple-element.100, f32[1,7680]{1,0:T(1,128)S(1)} %log1p.17, s32[]{:T(128)} %get-tuple-element.99, s32[]{:T(128)} %constant.52.clone.1..sunk) | dynamic-update-slice | bytes 61444 | tf_op jit(solution)/shard_map/while/body/jit(dynamic_update_index_in_dim)/dynamic_update_slice | solution.py:47
  45.5 0.7 dynamic_slice.31
  46.1 0.7 iota_compare_fusion.2
  46.8 7.7 %fusion.25 = f32[7680]{0:T(1024)S(1)} fusion(f32[7680]{0:T(1024)S(1)} %get-tuple-element.112, bf16[768,7680]{1,0:T(8,128)(2,1)} %get-tuple-element.111, pred[256]{0:T(512)(128)(4,1)S(1)} %iota_compare_fusion.2, bf16[6,256,768]{2,1,0:T(8,128)(2,1)} %get-tuple-element.110, s32[]{:T(128)} %get-tuple-element.99), kind=kOutput, calls=%fused_computation.3.clone.1 | convolution fusion | flops 3025789440 | bytes 12251904 | tf_op jit(solution)/shard_map/while/body/eval_jaxpr/dot_general | solution.py:42
  54.6 1.8 %dynamic_update_slice.5 = f32[6,7680]{1,0:T(8,128)} dynamic-update-slice(f32[6,7680]{1,0:T(8,128)} %get-tuple-element.100, f32[1,7680]{1,0:T(1,128)S(1)} %log1p.17, s32[]{:T(128)} %get-tuple-element.99, s32[]{:T(128)} %constant.52.clone.1..sunk) | dynamic-update-slice | bytes 61444 | tf_op jit(solution)/shard_map/while/body/jit(dynamic_update_index_in_dim)/dynamic_update_slice | solution.py:47
  56.4 0.7 dynamic_slice.31
  57.0 0.7 iota_compare_fusion.2
  57.7 7.7 %fusion.25 = f32[7680]{0:T(1024)S(1)} fusion(f32[7680]{0:T(1024)S(1)} %get-tuple-element.112, bf16[768,7680]{1,0:T(8,128)(2,1)} %get-tuple-element.111, pred[256]{0:T(512)(128)(4,1)S(1)} %iota_compare_fusion.2, bf16[6,256,768]{2,1,0:T(8,128)(2,1)} %get-tuple-element.110, s32[]{:T(128)} %get-tuple-element.99), kind=kOutput, calls=%fused_computation.3.clone.1 | convolution fusion | flops 3025789440 | bytes 12251904 | tf_op jit(solution)/shard_map/while/body/eval_jaxpr/dot_general | solution.py:42
  65.6 1.8 %dynamic_update_slice.5 = f32[6,7680]{1,0:T(8,128)} dynamic-update-slice(f32[6,7680]{1,0:T(8,128)} %get-tuple-element.100, f32[1,7680]{1,0:T(1,128)S(1)} %log1p.17, s32[]{:T(128)} %get-tuple-element.99, s32[]{:T(128)} %constant.52.clone.1..sunk) | dynamic-update-slice | bytes 61444 | tf_op jit(solution)/shard_map/while/body/jit(dynamic_update_index_in_dim)/dynamic_update_slice | solution.py:47
  67.3 0.7 dynamic_slice.31
  68.0 0.7 iota_compare_fusion.2
  68.7 7.7 %fusion.25 = f32[7680]{0:T(1024)S(1)} fusion(f32[7680]{0:T(1024)S(1)} %get-tuple-element.112, bf16[768,7680]{1,0:T(8,128)(2,1)} %get-tuple-element.111, pred[256]{0:T(512)(128)(4,1)S(1)} %iota_compare_fusion.2, bf16[6,256,768]{2,1,0:T(8,128)(2,1)} %get-tuple-element.110, s32[]{:T(128)} %get-tuple-element.99), kind=kOutput, calls=%fused_computation.3.clone.1 | convolution fusion | flops 3025789440 | bytes 12251904 | tf_op jit(solution)/shard_map/while/body/eval_jaxpr/dot_general | solution.py:42
  76.5 1.8 %dynamic_update_slice.5 = f32[6,7680]{1,0:T(8,128)} dynamic-update-slice(f32[6,7680]{1,0:T(8,128)} %get-tuple-element.100, f32[1,7680]{1,0:T(1,128)S(1)} %log1p.17, s32[]{:T(128)} %get-tuple-element.99, s32[]{:T(128)} %constant.52.clone.1..sunk) | dynamic-update-slice | bytes 61444 | tf_op jit(solution)/shard_map/while/body/jit(dynamic_update_index_in_dim)/dynamic_update_slice | solution.py:47
  78.2 0.7 dynamic_slice.31
  78.9 0.7 iota_compare_fusion.2
  79.6 7.7 %fusion.25 = f32[7680]{0:T(1024)S(1)} fusion(f32[7680]{0:T(1024)S(1)} %get-tuple-element.112, bf16[768,7680]{1,0:T(8,128)(2,1)} %get-tuple-element.111, pred[256]{0:T(512)(128)(4,1)S(1)} %iota_compare_fusion.2, bf16[6,256,768]{2,1,0:T(8,128)(2,1)} %get-tuple-element.110, s32[]{:T(128)} %get-tuple-element.99), kind=kOutput, calls=%fused_computation.3.clone.1 | convolution fusion | flops 3025789440 | bytes 12251904 | tf_op jit(solution)/shard_map/while/body/eval_jaxpr/dot_general | solution.py:42
  87.4 1.8 %dynamic_update_slice.5 = f32[6,7680]{1,0:T(8,128)} dynamic-update-slice(f32[6,7680]{1,0:T(8,128)} %get-tuple-element.100, f32[1,7680]{1,0:T(1,128)S(1)} %log1p.17, s32[]{:T(128)} %get-tuple-element.99, s32[]{:T(128)} %constant.52.clone.1..sunk) | dynamic-update-slice | bytes 61444 | tf_op jit(solution)/shard_map/while/body/jit(dynamic_update_index_in_dim)/dynamic_update_slice | solution.py:47
  89.1 0.7 dynamic_slice.31
  89.8 0.7 iota_compare_fusion.2
  90.5 7.7 %fusion.25 = f32[7680]{0:T(1024)S(1)} fusion(f32[7680]{0:T(1024)S(1)} %get-tuple-element.112, bf16[768,7680]{1,0:T(8,128)(2,1)} %get-tuple-element.111, pred[256]{0:T(512)(128)(4,1)S(1)} %iota_compare_fusion.2, bf16[6,256,768]{2,1,0:T(8,128)(2,1)} %get-tuple-element.110, s32[]{:T(128)} %get-tuple-element.99), kind=kOutput, calls=%fused_computation.3.clone.1 | convolution fusion | flops 3025789440 | bytes 12251904 | tf_op jit(solution)/shard_map/while/body/eval_jaxpr/dot_general | solution.py:42
  98.3 1.8 %dynamic_update_slice.5 = f32[6,7680]{1,0:T(8,128)} dynamic-update-slice(f32[6,7680]{1,0:T(8,128)} %get-tuple-element.100, f32[1,7680]{1,0:T(1,128)S(1)} %log1p.17, s32[]{:T(128)} %get-tuple-element.99, s32[]{:T(128)} %constant.52.clone.1..sunk) | dynamic-update-slice | bytes 61444 | tf_op jit(solution)/shard_map/while/body/jit(dynamic_update_index_in_dim)/dynamic_update_slice | solution.py:47
  100.0 11.3 %all-gather = f32[4,6,7680]{2,1,0:T(8,128)S(1)} all-gather(f32[1,6,7680]{2,1,0:T(8,128)} %bitcast.25), channel_id=1, replica_groups=mesh['grp'=2,'doc'=4,'voc'=4] {'doc'}, dimensions={0}, use_global_device_ids=true | all-gather | bytes 921600 | tf_op jit(solution)/shard_map/all_gather | solution.py:56
  111.4 1.0 reshape.54
  112.4 3.4 %copy.17 = f32[24,7680]{0,1:T(8,128)} copy(f32[24,7680]{1,0:T(8,128)} %reshape.54) | data formatting | bytes 1474560
  115.8 0.1 copy.18
  115.9 29.8 %gather_fusion = f32[8192,24]{1,0:T(8,128)} fusion(f32[24,7680]{0,1:T(8,128)} %copy.17, s32[8192]{0:T(1024)S(1)} %broadcast_clamp_fusion), kind=kCustom, calls=%fused_computation | custom fusion | bytes 1605632 | tf_op jit(solution)/shard_map/gather | solution.py:31
  145.7 3.0 %multiply_reduce_fusion.1 = f32[256,24]{1,0:T(8,128)S(1)} fusion(f32[256,32]{1,0:T(8,128)S(1)} %copy.18, f32[8192,24]{1,0:T(8,128)} %gather_fusion), kind=kLoop, calls=%fused_computation.29 | loop fusion | flops 387072 | bytes 843776 | tf_op jit(solution)/shard_map/reduce_sum | solution.py:32
  148.8 0.1 copy.19
  148.8 12.6 %fusion = f32[8,256]{1,0:T(8,128)S(1)} fusion(f32[24,256]{1,0:T(8,128)S(1)} %copy.19), kind=kCustom, calls=%all-reduce-scatter | all-reduce-scatter fusion | flops 8193 | bytes 33280
  161.5 2.9 %collective-permute-start = (f32[6,256]{1,0:T(8,128)S(1)}, f32[6,256]{1,0:T(8,128)S(1)}, u32[]{:S(2)}, u32[]{:S(2)}) collective-permute-start(f32[6,256]{1,0:T(8,128)S(1)} %slice.2), channel_id=1, source_target_pairs={{0,1},{1,2},{2,3},{4,5},{5,6},{6,7},{8,9},{9,10},{10,11},{12,13},{... | collective-permute-start | bytes 18440
  164.4 0.6 dynamic-slice.4
  165.7 0.1 collective-permute-done
  165.8 0.1 concatenate
  165.8 0.6 constant_dynamic-slice_fusion
  (27 shorter events, 0.3 us)
Async XLA Ops:
  0.0 2.1 %copy-start = (bf16[6,256,768]{2,1,0:T(8,128)(2,1)S(1)}, bf16[6,256,768]{2,1,0:T(8,128)(2,1)}, u32[]{:S(2)}) copy-start(bf16[6,256,768]{2,1,0:T(8,128)(2,1)} %param.12) | copy-start | bytes 7077892
  31.6 0.8 copy-start.1
  31.7 0.8 copy-start.2
  32.4 2.2 %copy-start.4 = (f32[7680]{0:T(1024)S(1)}, f32[7680]{0:T(1024)}, u32[]{:S(2)}) copy-start(f32[7680]{0:T(1024)} %param.19) | copy-start | bytes 92164
  32.4 2.2 %copy-start.5 = (s32[6]{0:T(128)S(1)}, s32[6]{0:T(128)}, u32[]{:S(2)}) copy-start(s32[6]{0:T(128)} %param.13) | copy-start | bytes 76
  145.7 18.7 %copy-start.3 = (u32[32]{0:T(128)S(1)}, u32[32]{0:T(128)}, u32[]{:S(2)}) copy-start(u32[32]{0:T(128)} %constant.110) | copy-start | bytes 388
  161.5 4.3 %collective-permute-start = (f32[6,256]{1,0:T(8,128)S(1)}, f32[6,256]{1,0:T(8,128)S(1)}, u32[]{:S(2)}, u32[]{:S(2)}) collective-permute-start(f32[6,256]{1,0:T(8,128)S(1)} %slice.2), channel_id=1, source_target_pairs={{0,1},{1,2},{2,3},{4,5},{5,6},{6,7},{8,9},{9,10},{10,11},{12,13},{... | collective-permute-start | bytes 18440
where the time goes:
time: 167 us; the launch traced here: 166 us
  matrix products  76 us (46%)
  local copies, waits for them, and re-layouts  50.4 us (30%)
  blocking collectives  24 us (14%)
  other arithmetic  12 us (7%)
  starting transfers between devices  2.94 us (2%)
    dot_general x6, matrix products, pool_rows(): jnp.dot(passage, w_decode, preferred_element_type=jnp.float32) + b_decode  46.5 us
    gather x1, local copies, waits for them, and re-layouts, score_rows(): picked = rows[:, local_ids]  29.8 us
    dot_general x1, matrix products, transform(): pre = jnp.dot(flat, w_trans, preferred_element_type=jnp.float32) + b_trans  29.6 us
    unnamed x1, blocking collectives  12.6 us
    all_gather x1, blocking collectives, shards(): lax.all_gather(impacts, 'doc', axis=0, tiled=True)  11.3 us
    dynamic_update_slice x6, local copies, waits for them, and re-layouts, shards(): impacts = lax.map(pool_rows, (transformed, lengths))  10.5 us
    unnamed x18, local copies, waits for them, and re-layouts  5.7 us
    lt x6, other arithmetic, pool_rows(): inside = jnp.arange(passage.shape[0], dtype=jnp.int32)[:, None] < live  4.15 us
  transfers between devices with their start and end apart: 1, of which 1 were waited for; matrix products, arithmetic and copies ran while one was open for 0% of the time, Pallas kernels for 0%

commit v1 on v0

v1 whole, which is shorter than its diff:
```python
import functools

import jax
import jax.numpy as jnp
from jax import lax
from jax.experimental import pallas as pl
from jax.experimental.pallas import tpu as pltpu
from jax.sharding import PartitionSpec as P

eps = 1e-06
score_scale = 1.0 / 1024.0
group = 16
chunk = 256


def pool_kernel(
    count, length, lens, hidden, w_trans, b_trans, gain, bias, w_decode, b_decode, out,
    kept, gathered, maxima, source, first
):
    per_chunk = chunk // group
    width = w_decode.shape[1]

    @pl.when(pl.program_id(0) == 0)
    def _():
        at = jnp.int32(0)
        for p in range(count):
            first[p] = at
            groups = (lens[p] + (group - 1)) // group

            def put(j, _, p=p, at=at):
                source[at + j] = p * length + j * group
                return 0

            lax.fori_loop(0, groups, put, 0)
            at = at + groups
        first[count] = at
        chunks = (at + (per_chunk - 1)) // per_chunk

        def pad(j, _):
            source[j] = 0
            return 0

        lax.fori_loop(at, chunks * per_chunk, pad, 0)

        def transform(c, _):
            for i in range(per_chunk):
                start = pl.multiple_of(source[c * per_chunk + i], group)
                gathered[i * group:(i + 1) * group, :] = hidden[pl.ds(start, group), :]
            pre = jnp.dot(gathered[...], w_trans[...], preferred_element_type=jnp.float32)
            pre = pre + b_trans[...]
            active = 0.5 * pre * (1.0 + lax.erf(pre * (0.5 ** 0.5)))
            centre = active - jnp.mean(active, -1, keepdims=True)
            spread = jnp.mean(centre * centre, -1, keepdims=True)
            normed = centre * lax.rsqrt(spread + eps) * gain[...] + bias[...]
            kept[pl.ds(pl.multiple_of(c * chunk, chunk), chunk), :] = normed.astype(jnp.bfloat16)
            return 0

        lax.fori_loop(0, chunks, transform, 0)
        for p in range(count):
            last = first[p + 1] - 1
            live = lens[p] - (last - first[p]) * group
            rows = pl.ds(pl.multiple_of(last * group, group), group)
            head = kept[pl.ds(pl.multiple_of(first[p] * group, group), group), :]
            head = head.astype(jnp.float32)[0:1, :]
            inside = lax.broadcasted_iota(jnp.int32, (group, kept.shape[1]), 0) < live
            fixed = jnp.where(inside, kept[rows, :].astype(jnp.float32), head)
            kept[rows, :] = fixed.astype(jnp.bfloat16)

    chunks = (first[count] + (per_chunk - 1)) // per_chunk

    def decode(c, _):
        rows = kept[pl.ds(pl.multiple_of(c * chunk, chunk), chunk), :]
        logits = jnp.dot(rows, w_decode[...], preferred_element_type=jnp.float32)
        tops = jnp.max(logits.reshape(per_chunk, group // 8, 8, width), 1)
        maxima[pl.ds(c * per_chunk, per_chunk)] = tops
        return 0

    lax.fori_loop(0, chunks, decode, 0)
    step = 4
    for p in range(count):
        start, last = first[p], first[p + 1] - 1

        def fold(j, top, start=start, last=last):
            for i in range(step):
                top = jnp.maximum(top, maxima[jnp.minimum(start + j * step + i, last)])
            return top

        trips = (last - start + step) // step
        top = lax.fori_loop(0, trips, fold, maxima[start])
        best = jnp.max(top, 0, keepdims=True) + b_decode[...]
        out[p:p + 1, :] = jnp.log1p(jnp.maximum(best, 0.0))


def tile_of(width):
    best = 128
    for tile in range(128, 1537, 128):
        if width % tile == 0:
            best = tile
    return best


def pool(hidden, lengths, w_trans, b_trans, ln_gain, ln_bias, w_decode, b_decode):
    count, length, features = hidden.shape
    terms = w_decode.shape[1]
    tile = tile_of(terms)
    rows = -(-count * length // chunk) * chunk
    whole = lambda shape: pl.BlockSpec(shape, lambda i, lens: (0, 0), pipeline_mode=pl.Buffered(1))
    return pl.pallas_call(
        functools.partial(pool_kernel, count, length),
        out_shape=jax.ShapeDtypeStruct((count, terms), jnp.float32),
        grid_spec=pltpu.PrefetchScalarGridSpec(
            num_scalar_prefetch=1,
            grid=(terms // tile,),
            in_specs=[
                whole((count * length, features)),
                whole((features, features)),
                whole((1, features)),
                whole((1, features)),
                whole((1, features)),
                pl.BlockSpec((features, tile), lambda i, lens: (0, i)),
                pl.BlockSpec((1, tile), lambda i, lens: (0, i)),
            ],
            out_specs=pl.BlockSpec((count, tile), lambda i, lens: (0, i)),
            scratch_shapes=[
                pltpu.VMEM((rows, features), jnp.bfloat16),
                pltpu.VMEM((chunk, features), jnp.bfloat16),
                pltpu.VMEM((rows // group, 8, tile), jnp.float32),
                pltpu.SMEM((rows // group,), jnp.int32),
                pltpu.SMEM((count + 1,), jnp.int32),
            ],
        ),
        compiler_params=pltpu.CompilerParams(
            dimension_semantics=("arbitrary",), vmem_limit_bytes=60 * 1024 * 1024
        ),
    )(
        lengths, hidden.reshape(count * length, features), w_trans, b_trans[None],
        ln_gain[None], ln_bias[None], w_decode, b_decode[None]
    )


def block_terms(query_ids, query_wts, start, width):
    local_ids = query_ids - start
    inside = (local_ids >= 0) & (local_ids < width)
    clipped = jnp.clip(local_ids, 0, width - 1)
    weights = jnp.where(inside, query_wts, 0).astype(jnp.float32)
    return (clipped, weights)


def score_rows(rows, local_ids, weights):
    picked = rows[:, local_ids]
    return jnp.sum(picked * weights[None], -1) * score_scale


def shards(
    hidden, lengths, w_trans, b_trans, ln_gain, ln_bias, w_decode, b_decode, query_ids, query_wts
):
    impacts = pool(hidden, lengths, w_trans, b_trans, ln_gain, ln_bias, w_decode, b_decode)
    term_width = w_decode.shape[1]
    term_start = lax.axis_index("voc") * term_width
    local_ids, weights = block_terms(query_ids, query_wts, term_start, term_width)
    own_count = query_ids.shape[0] // lax.axis_size("doc")
    own_start = lax.axis_index("doc") * own_count
    own_ids = lax.dynamic_slice_in_dim(local_ids, own_start, own_count, 0)
    own_weights = lax.dynamic_slice_in_dim(weights, own_start, own_count, 0)
    partial_value = score_rows(
        lax.all_gather(impacts, "doc", axis=0, tiled=True), own_ids, own_weights
    )
    return lax.psum_scatter(partial_value, "voc", scatter_dimension=0, tiled=True)


def solution(mesh):
    return jax.shard_map(
        shards,
        mesh=mesh,
        in_specs=(
            P(("grp", "doc"), None, None),
            P(("grp", "doc")),
            P(),
            P(),
            P(),
            P(),
            P(None, "voc"),
            P("voc"),
            P("grp", None),
            P("grp", None),
        ),
        out_specs=P(("grp", "voc"), "doc"),
        check_vma=False,
    )
```

time: 167 us -> 102 us (0.61)
  matrix products: 76 us -> 0 us
  Pallas kernels: 0 us -> 25.4 us
  local copies, waits for them, and re-layouts: 50.4 us -> 39.2 us
  other arithmetic: 12 us -> 4.76 us
  blocking collectives: 24 us -> 28.2 us
    dot_general x7 -> x0, matrix products: 76 us -> none  [the longest x6 46.5 us: pool_rows(): jnp.dot(passage, w_decode, preferred_element_type=jnp.float32) + b_decode]
    pallas_call x0 -> x1, Pallas kernels: none -> 25.4 us  [pool(): pl.pallas_call(functools.partial(pool_kernel, count, length), out_shape=j...]
    dynamic_update_slice x6 -> x0, local copies, waits for them, and re-layouts: 10.5 us -> none  [shards(): impacts = lax.map(pool_rows, (transformed, lengths))]
    broadcast_in_dim x0 -> x4, local copies, waits for them, and re-layouts: none -> 5.21 us  [the longest x1 1.39 us: pool(): b_decode[None]]
    all_gather x1, blocking collectives: 11.3 us -> 15.6 us  [shards(): lax.all_gather(impacts, 'doc', axis=0, tiled=True)]
    lt x6 -> x0, other arithmetic: 4.15 us -> none  [pool_rows(): inside = jnp.arange(passage.shape[0], dtype=jnp.int32)[:, None] < live]
    dynamic_slice x6 -> x0, local copies, waits for them, and re-layouts: 3.95 us -> none  [shards(): impacts = lax.map(pool_rows, (transformed, lengths))]
    convert_element_type x1 -> x0, other arithmetic: 2.13 us -> none  [transform(): return normed.astype(jnp.bfloat16).reshape(count, length, width)]
  transfers between devices with their start and end apart: 1 -> 1, of which waited for: 1 -> 1; matrix products, arithmetic and copies ran while one was open for 0% -> 1% of each run, Pallas kernels for 0% -> 0%
where the time goes in v1:
time: 102 us; the launch traced here: 101 us
  local copies, waits for them, and re-layouts  39.2 us (38%)
  blocking collectives  28.2 us (28%)
  Pallas kernels  25.4 us (25%)
  other arithmetic  4.76 us (5%)
  starting transfers between devices  2.94 us (3%)
    gather x1, local copies, waits for them, and re-layouts, score_rows(): picked = rows[:, local_ids]  29.8 us
    pallas_call x1, Pallas kernels, pool(): pl.pallas_call(functools.partial(pool_kernel, count, length), out_shape=j...  25.4 us
    all_gather x1, blocking collectives, shards(): lax.all_gather(impacts, 'doc', axis=0, tiled=True)  15.6 us
    unnamed x1, blocking collectives  12.6 us
    unnamed x8, local copies, waits for them, and re-layouts  3.88 us
    reduce_sum x1, other arithmetic, score_rows(): return jnp.sum(picked * weights[None], -1) * score_scale  3.04 us
    unnamed x1, starting transfers between devices  2.94 us
  transfers between devices with their start and end apart: 1, of which 1 were waited for; matrix products, arithmetic and copies ran while one was open for 1% of the time, Pallas kernels for 0%

profile of v1, /device:TPU:0, one launch (start us, length us, event | category | flops | bytes accessed | tf_op | source)
XLA Modules:
  0.0 101.4 jit_solution(4018583678093588739)
XLA Ops:
  0.0 0.9 broadcast_subtract_fusion
  0.9 0.8 compare_select_fusion
  1.7 0.1 copy.16
  1.8 0.1 reshape.7
  1.9 1.4 %broadcast_in_dim.21.b_decode = f32[1,7680]{1,0:T(1,128)} reshape(f32[7680]{0:T(1024)} %param.17) | data formatting | bytes 61440 | tf_op jit(solution)/shard_map/broadcast_in_dim | solution.py:137
  3.3 1.3 %broadcast_in_dim.18.b_trans = f32[1,768]{1,0:T(1,128)} reshape(f32[768]{0:T(1024)} %param.13) | data formatting | bytes 6144 | tf_op jit(solution)/shard_map/broadcast_in_dim | solution.py:136
  4.6 1.3 %broadcast_in_dim.19.gain = f32[1,768]{1,0:T(1,128)} reshape(f32[768]{0:T(1024)} %param.14) | data formatting | bytes 6144 | tf_op jit(solution)/shard_map/broadcast_in_dim | solution.py:137
  5.8 1.3 %broadcast_in_dim.20.bias = f32[1,768]{1,0:T(1,128)} reshape(f32[768]{0:T(1024)} %param.15) | data formatting | bytes 6144 | tf_op jit(solution)/shard_map/broadcast_in_dim | solution.py:137
  7.1 25.4 %shard_map.100 = f32[6,7680]{1,0:T(8,128)} custom-call(s32[6]{0:T(128)} %lens.1, bf16[1536,768]{1,0:T(8,128)(2,1)} %bitcast.9, bf16[768,768]{1,0:T(8,128)(2,1)} %w_trans.1, f32[1,768]{1,0:T(1,128)} %broadcast_in_dim.18.b_trans, f32[1,768]{1,0:T(1,128)} %broadcast_in_dim.19.gain, f32[1,768]{1,0:T(1,128)} %broadcast_in_dim.20.bias, ...), custom_call_target="tpu_custom_call" | custom-call | tf_op jit(solution)/shard_map/pallas_call | solution.py:108
  32.5 15.6 %all-gather = f32[4,6,7680]{2,1,0:T(8,128)S(1)} all-gather(f32[1,6,7680]{2,1,0:T(8,128)} %bitcast.10), channel_id=1, replica_groups=mesh['grp'=2,'doc'=4,'voc'=4] {'doc'}, dimensions={0}, use_global_device_ids=true | all-gather | bytes 921600 | tf_op jit(solution)/shard_map/all_gather | solution.py:166
  48.1 0.1 reshape.16
  48.2 2.5 %copy.17 = f32[24,7680]{0,1:T(8,128)} copy(f32[24,7680]{1,0:T(8,128)S(1)} %reshape.16) | data formatting | bytes 1474560
  50.7 0.1 copy.18
  50.8 29.8 %gather_fusion = f32[8192,24]{1,0:T(8,128)} fusion(f32[24,7680]{0,1:T(8,128)} %copy.17, s32[8192]{0:T(1024)S(1)} %broadcast_clamp_fusion), kind=kCustom, calls=%fused_computation | custom fusion | bytes 1605632 | tf_op jit(solution)/shard_map/gather | solution.py:150
  80.6 0.0 copy-start
  80.6 3.0 %multiply_reduce_fusion = f32[256,24]{1,0:T(8,128)S(1)} fusion(f32[256,32]{1,0:T(8,128)S(1)} %copy.18, f32[8192,24]{1,0:T(8,128)} %gather_fusion), kind=kLoop, calls=%fused_computation.1 | loop fusion | flops 387072 | bytes 843776 | tf_op jit(solution)/shard_map/reduce_sum | solution.py:151
  83.7 0.1 copy.19
  83.8 12.6 %fusion = f32[8,256]{1,0:T(8,128)S(1)} fusion(f32[24,256]{1,0:T(8,128)S(1)} %copy.19), kind=kCustom, calls=%all-reduce-scatter | all-reduce-scatter fusion | flops 8193 | bytes 33280
  96.4 2.9 %collective-permute-start = (f32[6,256]{1,0:T(8,128)S(1)}, f32[6,256]{1,0:T(8,128)S(1)}, u32[]{:S(2)}, u32[]{:S(2)}) collective-permute-start(f32[6,256]{1,0:T(8,128)S(1)} %slice.2), channel_id=1, source_target_pairs={{0,1},{1,2},{2,3},{4,5},{5,6},{6,7},{8,9},{9,10},{10,11},{12,13},{... | collective-permute-start | bytes 18440
  99.3 0.0 copy-done
  99.4 0.6 dynamic-slice.4
  100.6 0.1 collective-permute-done
  100.7 0.1 concatenate
  100.8 0.6 constant_dynamic-slice_fusion
  (3 shorter events, 0.0 us)
Async XLA Ops:
  80.6 18.7 %copy-start = (u32[32]{0:T(128)S(1)}, u32[32]{0:T(128)}, u32[]{:S(2)}) copy-start(u32[32]{0:T(128)} %constant.29) | copy-start | bytes 388
  96.4 4.3 %collective-permute-start = (f32[6,256]{1,0:T(8,128)S(1)}, f32[6,256]{1,0:T(8,128)S(1)}, u32[]{:S(2)}, u32[]{:S(2)}) collective-permute-start(f32[6,256]{1,0:T(8,128)S(1)} %slice.2), channel_id=1, source_target_pairs={{0,1},{1,2},{2,3},{4,5},{5,6},{6,7},{8,9},{9,10},{10,11},{12,13},{... | collective-permute-start | bytes 18440

commit v2 on v1

--- a/solution.py
+++ b/solution.py
@@ -47,11 +47,11 @@
                 start = pl.multiple_of(source[c * per_chunk + i], group)
                 gathered[i * group:(i + 1) * group, :] = hidden[pl.ds(start, group), :]
             pre = jnp.dot(gathered[...], w_trans[...], preferred_element_type=jnp.float32)
-            pre = pre + b_trans[...]
+            pre = pre + b_trans[...][None]
             active = 0.5 * pre * (1.0 + lax.erf(pre * (0.5 ** 0.5)))
             centre = active - jnp.mean(active, -1, keepdims=True)
             spread = jnp.mean(centre * centre, -1, keepdims=True)
-            normed = centre * lax.rsqrt(spread + eps) * gain[...] + bias[...]
+            normed = centre * lax.rsqrt(spread + eps) * gain[...][None] + bias[...][None]
             kept[pl.ds(pl.multiple_of(c * chunk, chunk), chunk), :] = normed.astype(jnp.bfloat16)
             return 0
 
@@ -76,6 +76,8 @@
         return 0
 
     lax.fori_loop(0, chunks, decode, 0)
+    offset = pl.multiple_of(pl.program_id(0) * width, width)
+    term_bias = b_decode[pl.ds(offset, width)][None]
     step = 4
     for p in range(count):
         start, last = first[p], first[p + 1] - 1
@@ -87,7 +89,7 @@
 
         trips = (last - start + step) // step
         top = lax.fori_loop(0, trips, fold, maxima[start])
-        best = jnp.max(top, 0, keepdims=True) + b_decode[...]
+        best = jnp.max(top, 0, keepdims=True) + term_bias
         out[p:p + 1, :] = jnp.log1p(jnp.maximum(best, 0.0))
 
 
@@ -105,6 +107,7 @@
     tile = tile_of(terms)
     rows = -(-count * length // chunk) * chunk
     whole = lambda shape: pl.BlockSpec(shape, lambda i, lens: (0, 0), pipeline_mode=pl.Buffered(1))
+    vector = pl.BlockSpec((features,), lambda i, lens: (0,), pipeline_mode=pl.Buffered(1))
     return pl.pallas_call(
         functools.partial(pool_kernel, count, length),
         out_shape=jax.ShapeDtypeStruct((count, terms), jnp.float32),
@@ -114,11 +117,9 @@
             in_specs=[
                 whole((count * length, features)),
                 whole((features, features)),
-                whole((1, features)),
-                whole((1, features)),
-                whole((1, features)),
+                vector, vector, vector,
                 pl.BlockSpec((features, tile), lambda i, lens: (0, i)),
-                pl.BlockSpec((1, tile), lambda i, lens: (0, i)),
+                pl.BlockSpec((terms,), lambda i, lens: (0,), pipeline_mode=pl.Buffered(1)),
             ],
             out_specs=pl.BlockSpec((count, tile), lambda i, lens: (0, i)),
             scratch_shapes=[
@@ -133,39 +134,190 @@
             dimension_semantics=("arbitrary",), vmem_limit_bytes=60 * 1024 * 1024
         ),
     )(
-        lengths, hidden.reshape(count * length, features), w_trans, b_trans[None],
-        ln_gain[None], ln_bias[None], w_decode, b_decode[None]
+        lengths, hidden.reshape(count * length, features), w_trans, b_trans, ln_gain, ln_bias,
+        w_decode, b_decode
     )
 
 
-def block_terms(query_ids, query_wts, start, width):
-    local_ids = query_ids - start
-    inside = (local_ids >= 0) & (local_ids < width)
-    clipped = jnp.clip(local_ids, 0, width - 1)
-    weights = jnp.where(inside, query_wts, 0).astype(jnp.float32)
-    return (clipped, weights)
-
-
-def score_rows(rows, local_ids, weights):
-    picked = rows[:, local_ids]
-    return jnp.sum(picked * weights[None], -1) * score_scale
+radix = 256
+pad = 8
+
+
+def score_kernel(
+    sizes, impacts, ids, wts, out,
+    slots, own_ids, own_wts, hi_at, lo_at, weight_at, table, part, parts,
+    load_sem, local_sem, doc_send, doc_recv, pass_send, pass_recv, voc_send, voc_recv
+):
+    docs, vocs = sizes
+    count, width = impacts.shape
+    slots_per, queries = own_ids.shape
+    per = radix // slots_per
+    leads = width // radix
+    grp, doc, voc = (lax.axis_index(name) for name in ("grp", "doc", "voc"))
+    mesh_ids = pl.DeviceIdType.MESH
+    partner = doc + 1 - 2 * lax.rem(doc, 2)
+
+    rows = pl.ds(pl.multiple_of(doc * queries, queries), queries)
+    loads = [
+        pltpu.make_async_copy(ids.at[:, rows], own_ids, load_sem.at[0]),
+        pltpu.make_async_copy(wts.at[:, rows], own_wts, load_sem.at[1]),
+    ]
+    for load in loads:
+        load.start()
+    slots[:, count:, :] = jnp.zeros((docs, pad - count, width), jnp.float32)
+
+    barrier = pltpu.get_barrier_semaphore()
+    near = [(grp, lax.rem(doc + 2 * j, docs), voc) for j in range(1, docs // 2)]
+    near.append((grp, partner, voc))
+    along = [(grp, doc, lax.rem(voc + j, vocs)) for j in range(1, vocs)]
+    for peer in near + along:
+        pl.semaphore_signal(barrier, inc=1, device_id=peer, device_id_type=mesh_ids)
+    pl.semaphore_wait(barrier, len(near) + len(along))
+
+    live = pl.ds(0, count)
+    sends = []
+    for j, peer in enumerate(near):
+        copy = pltpu.make_async_remote_copy(
+            src_ref=impacts, dst_ref=slots.at[doc, live], send_sem=doc_send.at[j],
+            recv_sem=doc_recv.at[j], device_id=peer, device_id_type=mesh_ids
+        )
+        copy.start()
+        sends.append(copy)
+    keep = pltpu.make_async_copy(impacts, slots.at[doc, live], local_sem)
+    keep.start()
+
+    for load in loads:
+        load.wait()
+    local = own_ids[...] - voc * width
+    lead = jnp.clip(local >> 8, -1, leads)
+    spread_to = (
+        lax.broadcasted_iota(jnp.int32, (slots_per, radix), 1) % slots_per
+        == lax.broadcasted_iota(jnp.int32, (slots_per, radix), 0)
+    ).astype(jnp.float32).astype(jnp.bfloat16)
+
+    def widen(value):
+        value = value.astype(jnp.float32).astype(jnp.bfloat16)
+        return lax.dot_general(
+            value, spread_to, (((0,), (0,)), ((), ())), preferred_element_type=jnp.float32
+        )
+
+    own = (
+        lax.broadcasted_iota(jnp.int32, (queries, radix), 0) % per
+        == lax.broadcasted_iota(jnp.int32, (queries, radix), 1) // slots_per
+    )
+    hi_at[...] = jnp.where(own, widen(lead), -1.0)
+    lo_at[...] = jnp.where(own, widen(local & (radix - 1)), 0.0)
+    weight_at[...] = widen(own_wts[...])
+
+    def build(g, _):
+        at = pl.ds(pl.multiple_of(g * per, per), per)
+        high, weight = hi_at[at, :], weight_at[at, :]
+        low = jnp.sum(lo_at[at, :], 0, keepdims=True)
+        spans = leads + leads % 2
+        left = jnp.concatenate(
+            [jnp.where(high == float(i), weight, 0.0) for i in range(spans)], 0
+        ).astype(jnp.bfloat16)
+        digits = lax.broadcasted_iota(jnp.int32, (radix, radix), 0).astype(jnp.float32)
+        right = jnp.where(digits == low, 1.0, 0.0).astype(jnp.bfloat16)
+        made = lax.dot_general(
+            left, right, (((1,), (1,)), ((), ())), preferred_element_type=jnp.float32
+        )
+        for i in range(leads):
+            table[at, i * radix:(i + 1) * radix] = made[i * per:(i + 1) * per]
+        return 0
+
+    groups = queries // per
+    early = groups * 3 // 4
+    lax.fori_loop(0, early, build, 0)
+    for copy in sends:
+        copy.wait()
+    passed = []
+    for j in range(1, docs // 2):
+        held = slots.at[lax.rem(doc + docs - 2 * j, docs), live]
+        copy = pltpu.make_async_remote_copy(
+            src_ref=held, dst_ref=held, send_sem=pass_send.at[j - 1],
+            recv_sem=pass_recv.at[j - 1], device_id=(grp, partner, voc), device_id_type=mesh_ids
+        )
+        copy.start()
+        passed.append(copy)
+    lax.fori_loop(early, groups, build, 0)
+    keep.wait()
+    for copy in passed:
+        copy.wait()
+
+    total = jnp.zeros((2 * docs * pad, queries), jnp.float32)
+    step = width // 5
+    for i in range(width // step):
+        cut = slice(i * step, (i + 1) * step)
+        value = slots[:, :, cut].reshape(docs * pad, step)
+        top = value.astype(jnp.bfloat16)
+        rest = (value - top.astype(jnp.float32)).astype(jnp.bfloat16)
+        pair = jnp.concatenate([top, rest], 0)
+        weight = table[:, cut]
+        big = weight.astype(jnp.bfloat16)
+        small = (weight - big.astype(jnp.float32)).astype(jnp.bfloat16)
+        for piece in (big, small):
+            total = total + lax.dot_general(
+                pair, piece, (((1,), (1,)), ((), ())), preferred_element_type=jnp.float32
+            )
+    total = (total[:docs * pad] + total[docs * pad:]) * score_scale
+    part[...] = total.reshape(docs, pad, queries)
+
+    share = docs // vocs
+    copies = []
+    for j, peer in enumerate(along):
+        copy = pltpu.make_async_remote_copy(
+            src_ref=part.at[pl.ds(peer[2] * share, share)], dst_ref=parts.at[j],
+            send_sem=voc_send.at[j], recv_sem=voc_recv.at[j], device_id=peer,
+            device_id_type=mesh_ids
+        )
+        copy.start()
+        copies.append(copy)
+    result = part[pl.ds(voc * share, share)]
+    for j, copy in enumerate(copies):
+        copy.wait()
+        result = result + parts[j]
+    for i in range(share):
+        out[i * count:(i + 1) * count, :] = result[i, :count]
+
+
+def score(impacts, ids, wts):
+    docs, vocs = lax.axis_size("doc"), lax.axis_size("voc")
+    count, width = impacts.shape
+    queries = ids.shape[1] // docs
+    anywhere = pl.BlockSpec(memory_space=pl.ANY)
+    inside = pl.BlockSpec(memory_space=pltpu.VMEM)
+    lanes = pltpu.VMEM((queries, radix), jnp.float32)
+    several = lambda n: pltpu.SemaphoreType.DMA((max(n, 1),))
+    return pl.pallas_call(
+        functools.partial(score_kernel, (docs, vocs)),
+        out_shape=jax.ShapeDtypeStruct((docs * count // vocs, queries), jnp.float32),
+        in_specs=[inside, anywhere, anywhere],
+        out_specs=inside,
+        scratch_shapes=[
+            pltpu.VMEM((docs, pad, width), jnp.float32),
+            pltpu.VMEM((ids.shape[0], queries), jnp.int32),
+            pltpu.VMEM((ids.shape[0], queries), jnp.int32),
+            lanes, lanes, lanes,
+            pltpu.VMEM((queries, width), jnp.float32),
+            pltpu.VMEM((docs, pad, queries), jnp.float32),
+            pltpu.VMEM((vocs - 1, docs // vocs, pad, queries), jnp.float32),
+            several(2), pltpu.SemaphoreType.DMA,
+            several(docs // 2), several(docs // 2),
+            several(docs // 2 - 1), several(docs // 2 - 1),
+            several(vocs - 1), several(vocs - 1),
+        ],
+        compiler_params=pltpu.CompilerParams(
+            collective_id=0, has_side_effects=True, vmem_limit_bytes=60 * 1024 * 1024
+        ),
+    )(impacts, ids, wts)
 
 
 def shards(
     hidden, lengths, w_trans, b_trans, ln_gain, ln_bias, w_decode, b_decode, query_ids, query_wts
 ):
     impacts = pool(hidden, lengths, w_trans, b_trans, ln_gain, ln_bias, w_decode, b_decode)
-    term_width = w_decode.shape[1]
-    term_start = lax.axis_index("voc") * term_width
-    local_ids, weights = block_terms(query_ids, query_wts, term_start, term_width)
-    own_count = query_ids.shape[0] // lax.axis_size("doc")
-    own_start = lax.axis_index("doc") * own_count
-    own_ids = lax.dynamic_slice_in_dim(local_ids, own_start, own_count, 0)
-    own_weights = lax.dynamic_slice_in_dim(weights, own_start, own_count, 0)
-    partial_value = score_rows(
-        lax.all_gather(impacts, "doc", axis=0, tiled=True), own_ids, own_weights
-    )
-    return lax.psum_scatter(partial_value, "voc", scatter_dimension=0, tiled=True)
+    return score(impacts, query_ids.T, query_wts.T)
 
 
 def solution(mesh):

time: 102 us -> 51.4 us (0.50)
  local copies, waits for them, and re-layouts: 39.2 us -> 1.3 us
  blocking collectives: 28.2 us -> 0 us
  Pallas kernels: 25.4 us -> 49.5 us
  other arithmetic: 4.76 us -> 0 us
  starting transfers between devices: 2.94 us -> 0 us
    gather x1 -> x0, local copies, waits for them, and re-layouts: 29.8 us -> none  [score_rows(): picked = rows[:, local_ids]]
    pallas_call x0 -> x1, Pallas kernels: none -> 24.1 us  [score(): pl.pallas_call(functools.partial(score_kernel, (docs, vocs)), out_shape=j...]
    all_gather x1 -> x0, blocking collectives: 15.6 us -> none  [shards(): lax.all_gather(impacts, 'doc', axis=0, tiled=True)]
    unnamed x1 -> x0, blocking collectives: 12.6 us -> none
    broadcast_in_dim x5 -> x0, local copies, waits for them, and re-layouts: 5.3 us -> none  [the longest x1 1.39 us: pool(): b_decode[None]]
    reduce_sum x1 -> x0, other arithmetic: 3.04 us -> none  [score_rows(): return jnp.sum(picked * weights[None], -1) * score_scale]
    unnamed x1 -> x0, starting transfers between devices: 2.94 us -> none
    unnamed x8 -> x1, local copies, waits for them, and re-layouts: 3.88 us -> 1.3 us
  transfers between devices with their start and end apart: 1 -> 0, of which waited for: 1 -> 0; matrix products, arithmetic and copies ran while one was open for 1% -> 0% of each run, Pallas kernels for 0% -> 0%
where the time goes in v2:
time: 51.4 us; the launch traced here: 50.8 us
  Pallas kernels  49.5 us (96%)
  local copies, waits for them, and re-layouts  1.3 us (3%)
    pallas_call x1, Pallas kernels, pool(): pl.pallas_call(functools.partial(pool_kernel, count, length), out_shape=j...  25.4 us
    pallas_call x1, Pallas kernels, score(): pl.pallas_call(functools.partial(score_kernel, (docs, vocs)), out_shape=j...  24.1 us
    unnamed x1, local copies, waits for them, and re-layouts  1.3 us

profile of v2, /device:TPU:0, one launch (start us, length us, event | category | flops | bytes accessed | tf_op | source)
XLA Modules:
  0.0 50.8 jit_solution(14905558345493045726)
XLA Ops:
  0.0 25.4 %shard_map.100.impacts = f32[6,7680]{1,0:T(8,128)} custom-call(s32[6]{0:T(128)} %lens.1, bf16[1536,768]{1,0:T(8,128)(2,1)} %bitcast.3, bf16[768,768]{1,0:T(8,128)(2,1)} %w_trans.1, f32[768]{0:T(1024)} %b_trans.1, f32[768]{0:T(1024)} %gain.1, f32[768]{0:T(1024)} %bias.1, bf16[768,7680]{1,0:T(8,128)(2,1)} %w_decode.1, f32[7680]{0:T(1024)} %b_decode.1), custom_call_target="tpu_custom_call" | custom-call | tf_op jit(solution)/shard_map/pallas_call | solution.py:111
  25.4 24.1 %shard_map.101 = f32[6,256]{1,0:T(8,128)} custom-call(f32[6,7680]{1,0:T(8,128)} %shard_map.100.impacts, s32[32,1024]{1,0:T(8,128)} %bitcast.4, s32[32,1024]{1,0:T(8,128)} %bitcast.5), custom_call_target="tpu_custom_call" | custom-call | tf_op jit(solution)/shard_map/pallas_call | solution.py:292
  49.5 1.3 %copy.12 = f32[6,256]{1,0:T(8,128)} copy(f32[6,256]{1,0:T(8,128)} %shard_map.101) | data formatting | bytes 12288

commit v3 on v0

v3 whole, which is shorter than its diff:
```python
import functools

import jax
import jax.numpy as jnp
from jax import lax
from jax.experimental import pallas as pl
from jax.experimental.pallas import tpu as pltpu
from jax.sharding import PartitionSpec as P

eps = 1e-06
score_scale = 1.0 / 1024.0
radix = 256
pad = 8


def tile_of(width):
    best = 128
    for tile in range(128, 1537, 128):
        if width % tile == 0:
            best = tile
    return best


def encode_kernel(
    sizes, count, tile, lens, b_trans, gain, bias, b_decode, hidden, w_trans, w_decode, ids, wts,
    out, states, mix, decoder, kept, slots, own_ids, own_wts, hi_at, lo_at, weight_at, table,
    part, parts, load_sem, state_sem, decoder_sem, doc_send, doc_recv, voc_send, voc_recv
):
    docs, vocs = sizes
    length, features = hidden.shape[0] // count, hidden.shape[1]
    width = w_decode.shape[1]
    tiles = width // tile
    slots_per, queries = own_ids.shape
    per = radix // slots_per
    leads = width // radix
    grp, doc, voc = (lax.axis_index(name) for name in ("grp", "doc", "voc"))
    mesh_ids = pl.DeviceIdType.MESH

    def state_load(p):
        rows = pl.ds(pl.multiple_of(p * length, length), length)
        return pltpu.make_async_copy(hidden.at[rows], states.at[rows], state_sem.at[p])

    def decoder_load(t):
        cut = pl.ds(pl.multiple_of(t * tile, tile), tile)
        return pltpu.make_async_copy(w_decode.at[:, cut], decoder.at[t], decoder_sem.at[t])

    mix_load = pltpu.make_async_copy(w_trans, mix, load_sem.at[0])
    mix_load.start()
    for p in range(count):
        state_load(p).start()
    rows = pl.ds(pl.multiple_of(doc * queries, queries), queries)
    loads = [
        pltpu.make_async_copy(ids.at[:, rows], own_ids, load_sem.at[1]),
        pltpu.make_async_copy(wts.at[:, rows], own_wts, load_sem.at[2]),
    ]
    for load in loads:
        load.start()
    for t in range(tiles):
        decoder_load(t).start()

    barrier = pltpu.get_barrier_semaphore()
    across = [(grp, lax.rem(doc + j, docs), voc) for j in range(1, docs)]
    along = [(grp, doc, lax.rem(voc + j, vocs)) for j in range(1, vocs)]
    for peer in across + along:
        pl.semaphore_signal(barrier, inc=1, device_id=peer, device_id_type=mesh_ids)
    mix_load.wait()

    def transform(p, _):
        state_load(p).wait()
        rows = pl.ds(pl.multiple_of(p * length, length), length)
        pre = jnp.dot(states[rows, :], mix[...], preferred_element_type=jnp.float32)
        pre = pre + b_trans[...][None]
        active = 0.5 * pre * (1.0 + lax.erf(pre * (0.5 ** 0.5)))
        centre = active - jnp.mean(active, -1, keepdims=True)
        spread = jnp.mean(centre * centre, -1, keepdims=True)
        normed = centre * lax.rsqrt(spread + eps) * gain[...][None] + bias[...][None]
        inside = lax.broadcasted_iota(jnp.int32, (length, features), 0) < lens[p]
        kept[rows, :] = jnp.where(inside, normed, normed[0:1]).astype(jnp.bfloat16)
        return 0

    lax.fori_loop(0, count, transform, 0)
    pl.semaphore_wait(barrier, len(across) + len(along))

    def share_copy(j, t):
        mine = slots.at[doc, t]
        return pltpu.make_async_remote_copy(
            src_ref=mine, dst_ref=mine, send_sem=doc_send.at[j, t], recv_sem=doc_recv.at[j, t],
            device_id=across[j], device_id_type=mesh_ids
        )

    def decode(t, _):
        decoder_load(t).wait()
        tops = []
        for p in range(count):
            logits = jnp.dot(
                kept[p * length:(p + 1) * length, :], decoder[t],
                preferred_element_type=jnp.float32
            )
            tops.append(jnp.max(logits, 0, keepdims=True))
        tops.append(jnp.zeros((pad - count, tile), jnp.float32))
        cut = pl.ds(pl.multiple_of(t * tile, tile), tile)
        best = jnp.concatenate(tops, 0) + b_decode[cut][None]
        slots[doc, t] = jnp.log1p(jnp.maximum(best, 0.0))
        for j in range(len(across)):
            share_copy(j, t).start()
        return 0

    lax.fori_loop(0, tiles, decode, 0)

    for load in loads:
        load.wait()
    local = own_ids[...] - voc * width
    lead = jnp.clip(local >> 8, -1, leads)
    spread_to = (
        lax.broadcasted_iota(jnp.int32, (slots_per, radix), 1) % slots_per
        == lax.broadcasted_iota(jnp.int32, (slots_per, radix), 0)
    ).astype(jnp.float32).astype(jnp.bfloat16)

    def widen(value):
        value = value.astype(jnp.float32).astype(jnp.bfloat16)
        return lax.dot_general(
            value, spread_to, (((0,), (0,)), ((), ())), preferred_element_type=jnp.float32
        )

    own = (
        lax.broadcasted_iota(jnp.int32, (queries, radix), 0) % per
        == lax.broadcasted_iota(jnp.int32, (queries, radix), 1) // slots_per
    )
    hi_at[...] = jnp.where(own, widen(lead), -1.0)
    lo_at[...] = jnp.where(own, widen(local & (radix - 1)), 0.0)
    weight_at[...] = widen(own_wts[...])

    def build(g, _):
        at = pl.ds(pl.multiple_of(g * per, per), per)
        high, weight = hi_at[at, :], weight_at[at, :]
        low = jnp.sum(lo_at[at, :], 0, keepdims=True)
        spans = leads + leads % 2
        left = jnp.concatenate(
            [jnp.where(high == float(i), weight, 0.0) for i in range(spans)], 0
        ).astype(jnp.bfloat16)
        digits = lax.broadcasted_iota(jnp.int32, (radix, radix), 0).astype(jnp.float32)
        right = jnp.where(digits == low, 1.0, 0.0).astype(jnp.bfloat16)
        made = lax.dot_general(
            left, right, (((1,), (1,)), ((), ())), preferred_element_type=jnp.float32
        )
        for i in range(leads):
            table[at, i * radix:(i + 1) * radix] = made[i * per:(i + 1) * per]
        return 0

    lax.fori_loop(0, queries // per, build, 0)

    def arrive(t, _):
        for j in range(len(across)):
            share_copy(j, t).wait()
        return 0

    lax.fori_loop(0, tiles, arrive, 0)

    total = jnp.zeros((2 * docs * pad, queries), jnp.float32)
    for t in range(tiles):
        value = slots[:, t].reshape(docs * pad, tile)
        top = value.astype(jnp.bfloat16)
        rest = (value - top.astype(jnp.float32)).astype(jnp.bfloat16)
        pair = jnp.concatenate([top, rest], 0)
        weight = table[:, t * tile:(t + 1) * tile]
        big = weight.astype(jnp.bfloat16)
        small = (weight - big.astype(jnp.float32)).astype(jnp.bfloat16)
        for piece in (big, small):
            total = total + lax.dot_general(
                pair, piece, (((1,), (1,)), ((), ())), preferred_element_type=jnp.float32
            )
    total = (total[:docs * pad] + total[docs * pad:]) * score_scale
    part[...] = total.reshape(docs, pad, queries)

    share = docs // vocs
    copies = []
    for j, peer in enumerate(along):
        copy = pltpu.make_async_remote_copy(
            src_ref=part.at[pl.ds(peer[2] * share, share)], dst_ref=parts.at[j],
            send_sem=voc_send.at[j], recv_sem=voc_recv.at[j], device_id=peer,
            device_id_type=mesh_ids
        )
        copy.start()
        copies.append(copy)
    result = part[pl.ds(voc * share, share)]
    for j, copy in enumerate(copies):
        copy.wait()
        result = result + parts[j]
    for i in range(share):
        out[i * count:(i + 1) * count, :] = result[i, :count]


def shards(
    hidden, lengths, w_trans, b_trans, ln_gain, ln_bias, w_decode, b_decode, query_ids, query_wts
):
    docs, vocs = lax.axis_size("doc"), lax.axis_size("voc")
    count, length, features = hidden.shape
    width = w_decode.shape[1]
    tile = tile_of(width)
    tiles = width // tile
    terms = query_ids.shape[1]
    queries = query_ids.shape[0] // docs
    anywhere = pl.BlockSpec(memory_space=pl.ANY)
    inside = pl.BlockSpec(memory_space=pltpu.VMEM)
    lanes = pltpu.VMEM((queries, radix), jnp.float32)
    queue = pltpu.SemaphoreType.DMA
    return pl.pallas_call(
        functools.partial(encode_kernel, (docs, vocs), count, tile),
        out_shape=jax.ShapeDtypeStruct((docs * count // vocs, queries), jnp.float32),
        in_specs=[pl.BlockSpec(memory_space=pltpu.SMEM)] + [inside] * 4 + [anywhere] * 5,
        out_specs=inside,
        scratch_shapes=[
            pltpu.VMEM((count * length, features), jnp.bfloat16),
            pltpu.VMEM((features, features), jnp.bfloat16),
            pltpu.VMEM((tiles, features, tile), jnp.bfloat16),
            pltpu.VMEM((count * length, features), jnp.bfloat16),
            pltpu.VMEM((docs, tiles, pad, tile), jnp.float32),
            pltpu.VMEM((terms, queries), jnp.int32),
            pltpu.VMEM((terms, queries), jnp.int32),
            lanes, lanes, lanes,
            pltpu.VMEM((queries, width), jnp.float32),
            pltpu.VMEM((docs, pad, queries), jnp.float32),
            pltpu.VMEM((vocs - 1, docs // vocs, pad, queries), jnp.float32),
            queue((3,)), queue((count,)), queue((tiles,)),
            queue((docs - 1, tiles)), queue((docs - 1, tiles)),
            queue((vocs - 1,)), queue((vocs - 1,)),
        ],
        compiler_params=pltpu.CompilerParams(
            collective_id=0, has_side_effects=True, vmem_limit_bytes=60 * 1024 * 1024
        ),
    )(
        lengths, b_trans, ln_gain, ln_bias, b_decode,
        hidden.reshape(count * length, features), w_trans, w_decode, query_ids.T, query_wts.T
    )


def solution(mesh):
    return jax.shard_map(
        shards,
        mesh=mesh,
        in_specs=(
            P(("grp", "doc"), None, None),
            P(("grp", "doc")),
            P(),
            P(),
            P(),
            P(),
            P(None, "voc"),
            P("voc"),
            P("grp", None),
            P("grp", None),
        ),
        out_specs=P(("grp", "voc"), "doc"),
        check_vma=False,
    )
```

time: 167 us -> 47.4 us (0.28)
  matrix products: 76 us -> 0 us
  local copies, waits for them, and re-layouts: 50.4 us -> 1.3 us
  Pallas kernels: 0 us -> 45.9 us
  blocking collectives: 24 us -> 0 us
  other arithmetic: 12 us -> 0 us
  starting transfers between devices: 2.94 us -> 0 us
    dot_general x7 -> x0, matrix products: 76 us -> none  [the longest x6 46.5 us: pool_rows(): jnp.dot(passage, w_decode, preferred_element_type=jnp.float32) + b_decode]
    pallas_call x0 -> x1, Pallas kernels: none -> 45.9 us  [shards(): pl.pallas_call(functools.partial(encode_kernel, (docs, vocs), count, tile...]
    gather x1 -> x0, local copies, waits for them, and re-layouts: 29.8 us -> none  [score_rows(): picked = rows[:, local_ids]]
    unnamed x1 -> x0, blocking collectives: 12.6 us -> none
    all_gather x1 -> x0, blocking collectives: 11.3 us -> none  [shards(): lax.all_gather(impacts, 'doc', axis=0, tiled=True)]
    dynamic_update_slice x6 -> x0, local copies, waits for them, and re-layouts: 10.5 us -> none  [shards(): impacts = lax.map(pool_rows, (transformed, lengths))]
    unnamed x18 -> x1, local copies, waits for them, and re-layouts: 5.7 us -> 1.3 us
    lt x6 -> x0, other arithmetic: 4.15 us -> none  [pool_rows(): inside = jnp.arange(passage.shape[0], dtype=jnp.int32)[:, None] < live]
  transfers between devices with their start and end apart: 1 -> 0, of which waited for: 1 -> 0; matrix products, arithmetic and copies ran while one was open for 0% -> 0% of each run, Pallas kernels for 0% -> 0%
where the time goes in v3:
time: 47.4 us; the launch traced here: 47.2 us
  Pallas kernels  45.9 us (97%)
  local copies, waits for them, and re-layouts  1.3 us (3%)
    pallas_call x1, Pallas kernels, shards(): pl.pallas_call(functools.partial(encode_kernel, (docs, vocs), count, tile...  45.9 us
    unnamed x1, local copies, waits for them, and re-layouts  1.3 us

profile of v3, /device:TPU:0, one launch (start us, length us, event | category | flops | bytes accessed | tf_op | source)
XLA Modules:
  0.0 47.2 jit_solution(2344820436563885184)
XLA Ops:
  0.0 45.9 %shard_map.100 = f32[6,256]{1,0:T(8,128)} custom-call(s32[6]{0:T(128)} %lens.1, f32[768]{0:T(1024)} %b_trans.1, f32[768]{0:T(1024)} %gain.1, f32[768]{0:T(1024)} %bias.1, f32[7680]{0:T(1024)} %b_decode.1, bf16[1536,768]{1,0:T(8,128)(2,1)} %bitcast.3, bf16[768,768]{1,0:T(8,128)(2,1)} %w_trans.1, bf16[768,7680]{1,0:T(8,128)(2,1)} %w_decode.1, ...), custom_call_target="tpu_custom_call" | custom-call | tf_op jit(solution)/shard_map/pallas_call | solution.py:207
  45.9 1.3 %copy.12 = f32[6,256]{1,0:T(8,128)} copy(f32[6,256]{1,0:T(8,128)} %shard_map.100) | data formatting | bytes 12288

commit v4 on v3

--- a/solution.py
+++ b/solution.py
@@ -81,6 +81,49 @@
     lax.fori_loop(0, count, transform, 0)
     pl.semaphore_wait(barrier, len(across) + len(along))
 
+    for load in loads:
+        load.wait()
+    local = own_ids[...] - voc * width
+    lead = jnp.clip(local >> 8, -1, leads)
+    spread_to = (
+        lax.broadcasted_iota(jnp.int32, (slots_per, radix), 1) % slots_per
+        == lax.broadcasted_iota(jnp.int32, (slots_per, radix), 0)
+    ).astype(jnp.float32).astype(jnp.bfloat16)
+
+    def widen(value):
+        value = value.astype(jnp.float32).astype(jnp.bfloat16)
+        return lax.dot_general(
+            value, spread_to, (((0,), (0,)), ((), ())), preferred_element_type=jnp.float32
+        )
+
+    own = (
+        lax.broadcasted_iota(jnp.int32, (queries, radix), 0) % per
+        == lax.broadcasted_iota(jnp.int32, (queries, radix), 1) // slots_per
+    )
+    hi_at[...] = jnp.where(own, widen(lead), -1.0)
+    lo_at[...] = jnp.where(own, widen(local & (radix - 1)), 0.0)
+    weight_at[...] = widen(own_wts[...])
+
+    def build(g, _):
+        at = pl.ds(pl.multiple_of(g * per, per), per)
+        high, weight = hi_at[at, :], weight_at[at, :]
+        low = jnp.sum(lo_at[at, :], 0, keepdims=True)
+        spans = leads + leads % 2
+        left = jnp.concatenate(
+            [jnp.where(high == float(i), weight, 0.0) for i in range(spans)], 0
+        ).astype(jnp.bfloat16)
+        digits = lax.broadcasted_iota(jnp.int32, (radix, radix), 0).astype(jnp.float32)
+        right = jnp.where(digits == low, 1.0, 0.0).astype(jnp.bfloat16)
+        made = lax.dot_general(
+            left, right, (((1,), (1,)), ((), ())), preferred_element_type=jnp.float32
+        )
+        for i in range(leads):
+            table[at, i * radix:(i + 1) * radix] = made[i * per:(i + 1) * per]
+        return 0
+
+    groups = queries // per
+    inner = groups * 5 // 8 // tiles
+
     def share_copy(j, t):
         mine = slots.at[doc, t]
         return pltpu.make_async_remote_copy(
@@ -90,6 +133,8 @@
 
     def decode(t, _):
         decoder_load(t).wait()
+        for i in range(inner):
+            build(t * inner + i, 0)
         tops = []
         for p in range(count):
             logits = jnp.dot(
@@ -107,47 +152,7 @@
 
     lax.fori_loop(0, tiles, decode, 0)
 
-    for load in loads:
-        load.wait()
-    local = own_ids[...] - voc * width
-    lead = jnp.clip(local >> 8, -1, leads)
-    spread_to = (
-        lax.broadcasted_iota(jnp.int32, (slots_per, radix), 1) % slots_per
-        == lax.broadcasted_iota(jnp.int32, (slots_per, radix), 0)
-    ).astype(jnp.float32).astype(jnp.bfloat16)
-
-    def widen(value):
-        value = value.astype(jnp.float32).astype(jnp.bfloat16)
-        return lax.dot_general(
-            value, spread_to, (((0,), (0,)), ((), ())), preferred_element_type=jnp.float32
-        )
-
-    own = (
-        lax.broadcasted_iota(jnp.int32, (queries, radix), 0) % per
-        == lax.broadcasted_iota(jnp.int32, (queries, radix), 1) // slots_per
-    )
-    hi_at[...] = jnp.where(own, widen(lead), -1.0)
-    lo_at[...] = jnp.where(own, widen(local & (radix - 1)), 0.0)
-    weight_at[...] = widen(own_wts[...])
-
-    def build(g, _):
-        at = pl.ds(pl.multiple_of(g * per, per), per)
-        high, weight = hi_at[at, :], weight_at[at, :]
-        low = jnp.sum(lo_at[at, :], 0, keepdims=True)
-        spans = leads + leads % 2
-        left = jnp.concatenate(
-            [jnp.where(high == float(i), weight, 0.0) for i in range(spans)], 0
-        ).astype(jnp.bfloat16)
-        digits = lax.broadcasted_iota(jnp.int32, (radix, radix), 0).astype(jnp.float32)
-        right = jnp.where(digits == low, 1.0, 0.0).astype(jnp.bfloat16)
-        made = lax.dot_general(
-            left, right, (((1,), (1,)), ((), ())), preferred_element_type=jnp.float32
-        )
-        for i in range(leads):
-            table[at, i * radix:(i + 1) * radix] = made[i * per:(i + 1) * per]
-        return 0
-
-    lax.fori_loop(0, queries // per, build, 0)
+    lax.fori_loop(inner * tiles, groups, build, 0)
 
     def arrive(t, _):
         for j in range(len(across)):

time: 47.4 us -> 44.7 us (0.943)
  Pallas kernels: 45.9 us -> 43.2 us
    pallas_call x1, Pallas kernels: 45.9 us -> 43.2 us  [shards(): pl.pallas_call(functools.partial(encode_kernel, (docs, vocs), count, tile...]
where the time goes in v4:
time: 44.7 us; the launch traced here: 44.5 us
  Pallas kernels  43.2 us (97%)
  local copies, waits for them, and re-layouts  1.3 us (3%)
    pallas_call x1, Pallas kernels, shards(): pl.pallas_call(functools.partial(encode_kernel, (docs, vocs), count, tile...  43.2 us
    unnamed x1, local copies, waits for them, and re-layouts  1.3 us

profile of v4, /device:TPU:0, one launch (start us, length us, event | category | flops | bytes accessed | tf_op | source)
XLA Modules:
  0.0 44.5 jit_solution(5031041407116833735)
XLA Ops:
  0.0 43.2 %shard_map.100 = f32[6,256]{1,0:T(8,128)} custom-call(s32[6]{0:T(128)} %lens.1, f32[768]{0:T(1024)} %b_trans.1, f32[768]{0:T(1024)} %gain.1, f32[768]{0:T(1024)} %bias.1, f32[7680]{0:T(1024)} %b_decode.1, bf16[1536,768]{1,0:T(8,128)(2,1)} %bitcast.3, bf16[768,768]{1,0:T(8,128)(2,1)} %w_trans.1, bf16[768,7680]{1,0:T(8,128)(2,1)} %w_decode.1, ...), custom_call_target="tpu_custom_call" | custom-call | tf_op jit(solution)/shard_map/pallas_call | solution.py:212
  43.2 1.3 %copy.12 = f32[6,256]{1,0:T(8,128)} copy(f32[6,256]{1,0:T(8,128)} %shard_map.100) | data formatting | bytes 12288
